TPU v7x, 32 devices: a whole 2x2x4 slice. The times are simulated.
32 devices in a mesh: lev: 4 (over x, core), gy: 8 (over z, y).
Axes of the slice: x: 2, y: 2, z: 4, core: 2. Of those that a mesh axis runs over, the one named last changes fastest.
Arguments:
- forcing: bfloat16 [4, 32, 768, 1024], P('lev', None, 'gy'), may hold values from -6 to 6
- spectral_weight: bfloat16 [2, 128, 32, 32, 128], P(None, 'gy'), may hold values from -4.1875 to 4.1875
- point_weight: bfloat16 [32, 32], replicated, may hold values from -1 to 1
- point_bias: float32 [32], replicated, may hold values from -3 to 3
- decoder: bfloat16 [4, 32], replicated, may hold values from -1 to 1
- coriolis: float32 [768], P('gy'), may hold values from -1.5 to 1.5
- layer_depth: float32 [4], replicated, may hold values from 0.5 to 2
Outputs:
- equilibrium: float32 [4, 32, 768, 1024], P('lev', None, 'gy')
- residual: float32 [3, 4, 768, 1024], P(None, 'lev', 'gy')
All inputs are finite; a program needn't handle non-finite values.
Results may differ from a plain program's by a relative error of at most 0.015.
Values may be sent and summed in bfloat16 or wider, within the bound.
No kernel may reach another device: no remote copies, remote signals or barrier semaphores. Data moves between devices by JAX's collectives and lax.ppermute only.
A program may use at most 128 MiB of HBM per device.

v0:
```python
import math
import jax
import jax.numpy as jnp
from jax import lax
from jax.sharding import PartitionSpec as P

ITERS = 3


def prefix(value, axis, combine, identity):
    peers, place = (lax.axis_size(axis), lax.axis_index(axis))
    everything = lax.all_gather(value, axis)
    start = jnp.broadcast_to(jnp.asarray(identity, value.dtype), value.shape)

    def hop(k, before):
        reached = k < place
        new = combine(before, everything[k])
        return jnp.where(reached, new, before)

    return lax.fori_loop(0, peers, hop, start)


def from_behind(value, axis, steps):
    count = lax.axis_size(axis)
    initial, last = (max(0, -steps), min(count, count - steps))
    return lax.ppermute(value, axis, [(source, source + steps) for source in range(initial, last)])


def extended(value, sides, width):
    for axis, dim in sides:
        peers, length = (lax.axis_size(axis), value.shape[dim])
        up = [(i, (i + 1) % peers) for i in range(peers)]
        down = [(j, i) for i, j in up]
        last = lax.slice_in_dim(value, length - width, length, axis=dim)
        initial = lax.slice_in_dim(value, 0, width, axis=dim)
        before = lax.ppermute(last, axis, up)
        after = lax.ppermute(initial, axis, down)
        value = jnp.concatenate([before, value, after], axis=dim)
    return value


def angles(row_index, col_index, length):
    phase = row_index[:, None] * col_index[None, :] % length
    return phase.astype(jnp.float32) * (2.0 * math.pi / length)


def signed_modes(length, count):
    index = jnp.arange(count, dtype=jnp.int32)
    return jnp.where(index < count // 2, index, index + (length - count))


def forward_x(length, count):
    turned = angles(jnp.arange(length, dtype=jnp.int32), jnp.arange(count, dtype=jnp.int32), length)
    return jnp.stack([jnp.cos(turned), -jnp.sin(turned)], 0).astype(jnp.bfloat16)


def forward_y(row_index, length, count):
    turned = angles(row_index, signed_modes(length, count), length)
    cosine = jnp.cos(turned)
    sine = jnp.sin(turned)
    return jnp.stack([jnp.stack([cosine, -sine], 1), jnp.stack([sine, cosine], 1)], 0).astype(
        jnp.bfloat16
    )


def inverse_y(row_index, length, count):
    turned = angles(signed_modes(length, count), row_index, length)
    cosine = jnp.cos(turned)
    sine = jnp.sin(turned)
    return jnp.stack([jnp.stack([cosine, sine], 1), jnp.stack([-sine, cosine], 1)], 0).astype(
        jnp.bfloat16
    )


def inverse_x(length, count, total):
    index = jnp.arange(count, dtype=jnp.int32)
    turned = angles(index, jnp.arange(length, dtype=jnp.int32), length)
    factor = jnp.where(index == 0, 1.0, 2.0).astype(jnp.float32)[:, None] / total
    return jnp.stack([factor * jnp.cos(turned), -factor * jnp.sin(turned)], 0).astype(jnp.bfloat16)


def mix_modes(spectrum, weights):
    real_part = spectrum[:, :, 0]
    imag_part = spectrum[:, :, 1]
    weight_real = weights[0].astype(jnp.float32)
    weight_imag = weights[1].astype(jnp.float32)
    highest = lax.Precision.HIGHEST
    out_real = jnp.einsum(
        "klim,kiom->klom", real_part, weight_real, precision=highest
    ) - jnp.einsum("klim,kiom->klom", imag_part, weight_imag, precision=highest)
    out_imag = jnp.einsum(
        "klim,kiom->klom", real_part, weight_imag, precision=highest
    ) + jnp.einsum("klim,kiom->klom", imag_part, weight_real, precision=highest)
    return jnp.stack([out_real, out_imag], 2).astype(jnp.bfloat16)


def add_terms(earlier, later):
    return earlier + later


def roll_diff(field, axis):
    return (jnp.roll(field, -1, axis) - jnp.roll(field, 1, axis)) * 0.5


def on_device(forcing, spectral_weight, point_weight, point_bias, decoder, coriolis, layer_depth):
    level_count, channels, row_count, cell_count = forcing.shape
    group_size = lax.axis_size("gy")
    total_rows = row_count * group_size
    own_mode_count = spectral_weight.shape[1]
    mode_count = own_mode_count * group_size
    ymode_count = spectral_weight.shape[4]
    every_row = jnp.arange(total_rows, dtype=jnp.int32)
    table_fx = forward_x(cell_count, mode_count)
    table_ix = inverse_x(cell_count, mode_count, cell_count * total_rows)
    source = forcing.astype(jnp.float32) + point_bias[None, :, None, None]
    current = forcing
    updated = source
    for iteration in range(ITERS):
        near_modes = jnp.einsum(
            "lcyx,rxk->lrcky", current, table_fx, preferred_element_type=jnp.float32
        ).astype(jnp.bfloat16)
        all_rows = lax.all_to_all(near_modes, "gy", split_axis=3, concat_axis=4, tiled=True)
        table_fy = forward_y(every_row, total_rows, ymode_count)
        spectrum = jnp.einsum(
            "lrcky,ryqm->klqcm", all_rows, table_fy, preferred_element_type=jnp.float32
        )
        mixed = mix_modes(spectrum, spectral_weight)
        table_iy = inverse_y(every_row, total_rows, ymode_count)
        back_rows = jnp.einsum(
            "klqcm,qmry->lrcky", mixed, table_iy, preferred_element_type=jnp.float32
        ).astype(jnp.bfloat16)
        own_modes = lax.all_to_all(back_rows, "gy", split_axis=4, concat_axis=3, tiled=True)
        spread = jnp.einsum(
            "lrcky,rkx->lcyx", own_modes, table_ix, preferred_element_type=jnp.float32
        )
        pointwise = jnp.einsum(
            "lcyx,co->loyx", current, point_weight, preferred_element_type=jnp.float32
        )
        updated = jax.nn.gelu(spread + pointwise + source, approximate=True)
        current = updated.astype(jnp.bfloat16)
    fields = jnp.einsum(
        "lcyx,fc->flyx", updated, decoder.astype(jnp.float32), precision=lax.Precision.HIGHEST
    )
    turning = coriolis[:, None]
    east_wind = fields[0]
    north_wind = fields[1]
    upward = fields[2]
    heat = fields[3]
    level_start = lax.axis_index("lev") * level_count
    own_depth = lax.dynamic_slice_in_dim(layer_depth, level_start, level_count, 0)
    inside = jnp.cumsum(own_depth[:, None, None] * heat, axis=0)
    lower_sum = prefix(inside[-1], "lev", add_terms, jnp.zeros_like(inside[-1]))
    geopotential = inside + lower_sum[None]
    lower_wind = from_behind(upward[-1], "lev", 1)
    below_level = jnp.concatenate([lower_wind[None], upward[:-1]], 0)
    rimmed = extended(jnp.stack([north_wind, geopotential], 0), (("gy", 2),), 1)
    along_y = (rimmed[:, :, 2:, :] - rimmed[:, :, :-2, :]) * 0.5
    continuity = roll_diff(east_wind, 2) + along_y[0] + upward - below_level
    balance_x = turning * north_wind - roll_diff(geopotential, 2)
    balance_y = turning * east_wind + along_y[1]
    residual = jnp.stack([continuity, balance_x, balance_y], 0)
    return (updated, residual)


def solution(mesh):
    return jax.shard_map(
        on_device,
        mesh=mesh,
        in_specs=(
            P("lev", None, "gy", None),
            P(None, "gy", None, None, None),
            P(),
            P(),
            P(),
            P("gy"),
            P(),
        ),
        out_specs=(P("lev", None, "gy", None), P(None, "lev", "gy", None)),
        check_vma=False,
    )
```

profile of v0, /device:TPU:1, one launch (start us, length us, event | category | flops | bytes accessed | tf_op | source)
XLA Modules:
  0.0 566.0 jit_solution(12187804742954895769)
XLA Ops:
  9.4 4.7 fusion.67
  17.0 6.6 %all-to-all-start = ((bf16[1,2,32,128,96]{4,2,1,0,3:T(8,128)(2,1)}), bf16[1,2,32,128,96]{4,2,1,0,3:T(8,128)(2,1)S(1)}, u32[]{:S(2)}, u32[]{:S(2)}) async-start(bf16[1,2,32,128,96]{4,2,1,0,3:T(8,128)(2,1)} %copy.119), calls=%async_computation | async-start | bytes 4194304 | tf_op jit(solution)/shard_map/all_to_all | solution.py:122
  28.0 42.9 %all-to-all-done = bf16[1,2,32,128,96]{4,2,1,0,3:T(8,128)(2,1)S(1)} async-done(((bf16[1,2,32,128,96]{4,2,1,0,3:T(8,128)(2,1)}), bf16[1,2,32,128,96]{4,2,1,0,3:T(8,128)(2,1)S(1)}, u32[]{:S(2)}, u32[]{:S(2)}) %all-to-all-start) | async-done | bytes 1572896 | tf_op jit(solution)/shard_map/all_to_all | solution.py:122
  77.7 5.1 fusion.31
  83.5 9.2 %copy.122 = bf16[1,2,32,16,768]{2,3,1,0,4:T(8,128)(2,1)} copy(bf16[1,2,32,16,768]{4,2,3,1,0:T(8,128)(2,1)S(1)} %fusion.58) | data formatting | bytes 3145728 | tf_op jit(solution)/shard_map/convert_element_type | solution.py:131
  92.6 9.5 %reshape.756 = bf16[8,2,49152]{2,1,0:T(2,128)(2,1)} reshape(bf16[768,1,2,16,32]{4,3,2,1,0:T(8,128)(2,1)} %bitcast.368) | data formatting | bytes 3145728
  102.1 4.9 all-to-all-start.1
  110.0 16.3 %fusion.47 = f32[32,96,1024]{2,0,1:T(8,128)} fusion(bf16[32,96,1024]{2,1,0:T(8,128)(2,1)} %bitcast.383, bf16[32,32]{1,0:T(8,128)(2,1)S(1)} %copy-done), kind=kOutput, calls=%fused_computation.70 | convolution fusion | flops 201326592 | bytes 18876416 | tf_op jit(solution)/shard_map/lcyx,co->loyx/dot_general | solution.py:136
  126.3 17.0 %all-to-all-done.1 = bf16[8,2,49152]{2,1,0:T(2,128)(2,1)S(1)} async-done(((bf16[8,2,49152]{2,1,0:T(2,128)(2,1)}), bf16[8,2,49152]{2,1,0:T(2,128)(2,1)S(1)}, u32[]{:S(2)}, u32[]{:S(2)}) %all-to-all-start.1) | async-done | bytes 1572896 | tf_op jit(solution)/shard_map/all_to_all | solution.py:132
  143.3 5.3 reshape.757
  148.7 8.5 %copy.123 = bf16[1,2,32,16,8,96]{5,3,4,2,1,0:T(8,128)(2,1)S(1)} copy(bf16[1,2,32,16,8,96]{2,3,1,5,4,0:T(8,128)(2,1)} %bitcast.369) | data formatting | bytes 3145728 | tf_op jit(solution)/shard_map/all_to_all | solution.py:132
  157.2 16.4 %fusion.7 = bf16[1,32,96,1024]{3,2,1,0:T(8,128)(2,1)S(1)} fusion(f32[32,96,1024]{2,0,1:T(8,128)} %fusion.47, bf16[1,32,96,1024]{3,2,1,0:T(8,128)(2,1)} %param.9, f32[32]{0:T(128)S(1)} %copy-done.13, bf16[2,32,128,96]{3,2,1,0:T(8,128)(2,1)S(1)} %bitcast.387, bf16[1,128,1024]{2,1,0:T(8,128)(2,1)} %get-tuple-element.164, ...), kind=kOutput, calls=%fused_computation.23 | convolution fusion | flops 1651769344 | bytes 27263104 | tf_op jit(solution)/shard_map/lrcky,rkx->lcyx/dot_general | solution.py:133
  182.7 51.9 %all_to_all.90 = bf16[1,2,32,128,96]{4,2,1,0,3:T(8,128)(2,1)S(1)} all-to-all(bf16[1,2,32,128,96]{4,2,1,0,3:T(8,128)(2,1)S(1)} %copy.128), channel_id=1, replica_groups=mesh['lev'=4,'gy'=8] {'gy'}, dimensions={3} | all-to-all | bytes 3145728 | tf_op jit(solution)/shard_map/all_to_all | solution.py:122
  241.3 5.1 fusion.33
  247.1 9.2 %copy.131 = bf16[1,2,32,16,768]{2,3,1,0,4:T(8,128)(2,1)} copy(bf16[1,2,32,16,768]{4,2,3,1,0:T(8,128)(2,1)S(1)} %fusion.59) | data formatting | bytes 3145728 | tf_op jit(solution)/shard_map/convert_element_type | solution.py:131
  256.3 9.5 %reshape.758 = bf16[8,2,49152]{2,1,0:T(2,128)(2,1)} reshape(bf16[768,1,2,16,32]{4,3,2,1,0:T(8,128)(2,1)} %bitcast.370) | data formatting | bytes 3145728
  270.3 11.6 %fusion.45 = f32[96,1024,32]{1,2,0:T(8,128)} fusion(bf16[32,96,1024]{2,1,0:T(8,128)(2,1)} %bitcast.385, bf16[32,32]{1,0:T(8,128)(2,1)S(1)} %copy-done), kind=kOutput, calls=%fused_computation.68 | convolution fusion | flops 201326592 | bytes 18876416 | tf_op jit(solution)/shard_map/lcyx,co->loyx/dot_general | solution.py:136
  281.9 24.2 %all-to-all-done.3 = bf16[8,2,49152]{2,1,0:T(2,128)(2,1)S(1)} async-done(((bf16[8,2,49152]{2,1,0:T(2,128)(2,1)}), bf16[8,2,49152]{2,1,0:T(2,128)(2,1)S(1)}, u32[]{:S(2)}, u32[]{:S(2)}) %all-to-all-start.3) | async-done | bytes 1572896 | tf_op jit(solution)/shard_map/all_to_all | solution.py:132
  306.0 5.3 reshape.759
  311.4 8.5 %copy.132 = bf16[1,2,32,16,8,96]{5,3,4,2,1,0:T(8,128)(2,1)S(1)} copy(bf16[1,2,32,16,8,96]{2,3,1,5,4,0:T(8,128)(2,1)} %bitcast.371) | data formatting | bytes 3145728 | tf_op jit(solution)/shard_map/all_to_all | solution.py:132
  319.9 16.4 %fusion.15 = bf16[1,32,96,1024]{3,2,1,0:T(8,128)(2,1)S(1)} fusion(f32[96,1024,32]{1,2,0:T(8,128)} %fusion.45, bf16[1,32,96,1024]{3,2,1,0:T(8,128)(2,1)} %param.9, f32[32]{0:T(128)S(1)} %copy-done.13, bf16[2,32,128,96]{3,2,1,0:T(8,128)(2,1)S(1)} %bitcast.388, bf16[1,128,1024]{2,1,0:T(8,128)(2,1)} %get-tuple-element.164, ...), kind=kOutput, calls=%fused_computation.31 | convolution fusion | flops 1651769344 | bytes 27263104 | tf_op jit(solution)/shard_map/lrcky,rkx->lcyx/dot_general | solution.py:133
  345.3 52.0 %all_to_all.91 = bf16[1,2,32,128,96]{4,2,1,0,3:T(8,128)(2,1)S(1)} all-to-all(bf16[1,2,32,128,96]{4,2,1,0,3:T(8,128)(2,1)S(1)} %copy.137), channel_id=1, replica_groups=mesh['lev'=4,'gy'=8] {'gy'}, dimensions={3} | all-to-all | bytes 3145728 | tf_op jit(solution)/shard_map/all_to_all | solution.py:122
  404.1 5.1 fusion.35
  409.9 9.2 %copy.140 = bf16[1,2,32,16,768]{2,3,1,0,4:T(8,128)(2,1)} copy(bf16[1,2,32,16,768]{4,2,3,1,0:T(8,128)(2,1)S(1)} %fusion.60) | data formatting | bytes 3145728 | tf_op jit(solution)/shard_map/convert_element_type | solution.py:131
  419.1 9.5 %reshape.760 = bf16[8,2,49152]{2,1,0:T(2,128)(2,1)} reshape(bf16[768,1,2,16,32]{4,3,2,1,0:T(8,128)(2,1)} %bitcast.372) | data formatting | bytes 3145728
  433.9 11.6 %fusion.43 = f32[96,1024,32]{1,2,0:T(8,128)} fusion(bf16[32,96,1024]{2,1,0:T(8,128)(2,1)} %bitcast.384, bf16[32,32]{1,0:T(8,128)(2,1)S(1)} %copy-done), kind=kOutput, calls=%fused_computation.66 | convolution fusion | flops 201326592 | bytes 18876416 | tf_op jit(solution)/shard_map/lcyx,co->loyx/dot_general | solution.py:136
  445.5 23.2 %all-to-all-done.5 = bf16[8,2,49152]{2,1,0:T(2,128)(2,1)S(1)} async-done(((bf16[8,2,49152]{2,1,0:T(2,128)(2,1)}), bf16[8,2,49152]{2,1,0:T(2,128)(2,1)S(1)}, u32[]{:S(2)}, u32[]{:S(2)}) %all-to-all-start.5) | async-done | bytes 1572896 | tf_op jit(solution)/shard_map/all_to_all | solution.py:132
  468.7 5.3 reshape.761
  474.0 8.5 %copy.141 = bf16[1,2,32,16,8,96]{5,3,4,2,1,0:T(8,128)(2,1)S(1)} copy(bf16[1,2,32,16,8,96]{2,3,1,5,4,0:T(8,128)(2,1)} %bitcast.373) | data formatting | bytes 3145728 | tf_op jit(solution)/shard_map/all_to_all | solution.py:132
  482.6 17.6 %fusion.22 = f32[1,32,96,1024]{3,2,1,0:T(8,128)S(1)} fusion(f32[96,1024,32]{1,2,0:T(8,128)} %fusion.43, bf16[1,32,96,1024]{3,2,1,0:T(8,128)(2,1)} %param.9, f32[32]{0:T(128)S(1)} %copy-done.13, bf16[2,32,128,96]{3,2,1,0:T(8,128)(2,1)S(1)} %bitcast.386, bf16[1,128,1024]{2,1,0:T(8,128)(2,1)S(1)} %copy-done.8, bf16[1,128,1024]{2,1,0:T(8,128)(2,1)S(1)} %copy-done.9), kind=kOutput, calls=%fused_computation.38 | convolution fusion | flops 1648623616 | bytes 33554560 | tf_op jit(solution)/shard_map/lrcky,rkx->lcyx/dot_general | solution.py:133
  500.2 11.3 %fusion.23 = f32[96,1024,4]{1,2,0:T(4,128)S(1)} fusion(f32[32,96,1024]{2,1,0:T(8,128)S(1)} %bitcast.379, bf16[4,32]{1,0:T(4,128)(2,1)S(1)} %copy-done.10), kind=kOutput, calls=%fused_computation.45 | convolution fusion | flops 150994944 | bytes 14156032 | tf_op jit(solution)/shard_map/lcyx,fc->flyx/dot_general | solution.py:141
  514.0 20.7 %all-gather.2.cloned.1.call-done = f32[4,96,1024]{2,1,0:T(8,128)} async-done(((f32[1,96,1024]{2,1,0:T(8,128)}), f32[4,96,1024]{2,1,0:T(8,128)}) %all-gather.2.cloned.1.call-update) | async-done | bytes 1572880 | tf_op jit(solution)/shard_map/all_gather | solution.py:12
  (95 shorter events, 93.5 us)
Async XLA Ops:
  7.2 102.8 %copy-start = (bf16[32,32]{1,0:T(8,128)(2,1)S(1)}, bf16[32,32]{1,0:T(8,128)(2,1)}, u32[]{:S(2)}) copy-start(bf16[32,32]{1,0:T(8,128)(2,1)} %param.11) | copy-start | bytes 6148
  9.4 4.7 copy-start.5
  17.0 54.0 %all-to-all-start = ((bf16[1,2,32,128,96]{4,2,1,0,3:T(8,128)(2,1)}), bf16[1,2,32,128,96]{4,2,1,0,3:T(8,128)(2,1)S(1)}, u32[]{:S(2)}, u32[]{:S(2)}) async-start(bf16[1,2,32,128,96]{4,2,1,0,3:T(8,128)(2,1)} %copy.119), calls=%async_computation | async-start | bytes 4194304 | tf_op jit(solution)/shard_map/all_to_all | solution.py:122
  102.1 41.2 %all-to-all-start.1 = ((bf16[8,2,49152]{2,1,0:T(2,128)(2,1)}), bf16[8,2,49152]{2,1,0:T(2,128)(2,1)S(1)}, u32[]{:S(2)}, u32[]{:S(2)}) async-start(bf16[8,2,49152]{2,1,0:T(2,128)(2,1)} %reshape.756), calls=%async_computation.1 | async-start | bytes 3145728 | tf_op jit(solution)/shard_map/all_to_all | solution.py:132
  126.3 30.9 %copy-start.13 = (f32[32]{0:T(128)S(1)}, f32[32]{0:T(128)}, u32[]{:S(2)}) copy-start(f32[32]{0:T(128)} %param.12) | copy-start | bytes 388
  157.2 19.1 %copy-start.6 = (bf16[1,1024,128]{2,1,0:T(8,128)(2,1)S(1)}, bf16[1,1024,128]{2,1,0:T(8,128)(2,1)}, u32[]{:S(2)}) copy-start(bf16[1,1024,128]{2,1,0:T(8,128)(2,1)} %copy-done.5) | copy-start | bytes 786436
  173.7 2.6 copy-start.3
  265.8 40.2 %all-to-all-start.3 = ((bf16[8,2,49152]{2,1,0:T(2,128)(2,1)}), bf16[8,2,49152]{2,1,0:T(2,128)(2,1)S(1)}, u32[]{:S(2)}, u32[]{:S(2)}) async-start(bf16[8,2,49152]{2,1,0:T(2,128)(2,1)} %reshape.758), calls=%async_computation.3 | async-start | bytes 3145728 | tf_op jit(solution)/shard_map/all_to_all | solution.py:132
  319.9 19.1 %copy-start.7 = (bf16[1,1024,128]{2,1,0:T(8,128)(2,1)S(1)}, bf16[1,1024,128]{2,1,0:T(8,128)(2,1)}, u32[]{:S(2)}) copy-start(bf16[1,1024,128]{2,1,0:T(8,128)(2,1)} %copy-done.5) | copy-start | bytes 786436
  336.3 2.6 copy-start.2
  419.1 14.2 %copy-start.12 = (f32[4]{0:T(128)S(1)}, f32[4]{0:T(128)}, u32[]{:S(2)}) copy-start(f32[4]{0:T(128)} %param.15) | copy-start | bytes 52
  428.6 40.1 %all-to-all-start.5 = ((bf16[8,2,49152]{2,1,0:T(2,128)(2,1)}), bf16[8,2,49152]{2,1,0:T(2,128)(2,1)S(1)}, u32[]{:S(2)}, u32[]{:S(2)}) async-start(bf16[8,2,49152]{2,1,0:T(2,128)(2,1)} %reshape.760), calls=%async_computation.5 | async-start | bytes 3145728 | tf_op jit(solution)/shard_map/all_to_all | solution.py:132
  432.8 101.9 %all-gather.2.cloned.1.call-start = ((), (), s32[]{:S(2)}) async-start(), calls=%async_computation.6 | async-start | bytes 1966080 | tf_op jit(solution)/shard_map/all_gather | solution.py:12
  445.5 37.0 %copy-start.8 = (bf16[1,128,1024]{2,1,0:T(8,128)(2,1)S(1)}, bf16[1,128,1024]{2,1,0:T(8,128)(2,1)}, u32[]{:S(2)}) copy-start(bf16[1,128,1024]{2,1,0:T(8,128)(2,1)} %get-tuple-element.164) | copy-start | bytes 786436
  445.5 37.0 %copy-start.9 = (bf16[1,128,1024]{2,1,0:T(8,128)(2,1)S(1)}, bf16[1,128,1024]{2,1,0:T(8,128)(2,1)}, u32[]{:S(2)}) copy-start(bf16[1,128,1024]{2,1,0:T(8,128)(2,1)} %get-tuple-element.165) | copy-start | bytes 786436
  482.5 17.6 %copy-start.10 = (bf16[4,32]{1,0:T(4,128)(2,1)S(1)}, bf16[4,32]{1,0:T(4,128)(2,1)}, u32[]{:S(2)}) copy-start(bf16[4,32]{1,0:T(4,128)(2,1)} %param.13) | copy-start | bytes 772
  500.2 11.3 %copy-start.1 = (f32[1,32,96,1024]{3,2,1,0:T(8,128)}, f32[1,32,96,1024]{3,2,1,0:T(8,128)S(1)}, u32[]{:S(2)}) copy-start(f32[1,32,96,1024]{3,2,1,0:T(8,128)S(1)} %fusion.22) | copy-start | bytes 37748740
  514.0 25.3 %copy-start.4 = (f32[1,96,1024]{2,1,0:T(8,128)S(1)}, f32[1,96,1024]{2,1,0:T(8,128)}, u32[]{:S(2)}) copy-start(f32[1,96,1024]{2,1,0:T(8,128)} %get-tuple-element.137) | copy-start | bytes 1179652
  514.0 34.8 %copy-start.11 = (f32[96]{0:T(128)S(1)}, f32[96]{0:T(128)}, u32[]{:S(2)}) copy-start(f32[96]{0:T(128)} %param.14) | copy-start | bytes 1156
  539.5 4.8 collective-permute-start
  543.5 5.2 collective-permute-start.1
  549.1 8.5 %collective-permute-start.2 = (f32[96,1024]{1,0:T(8,128)S(1)}, f32[96,1024]{1,0:T(8,128)S(1)}, u32[]{:S(2)}, u32[]{:S(2)}) collective-permute-start(f32[96,1024]{1,0:T(8,128)S(1)} %get-tuple-element.135), channel_id=1, source_target_pairs={{0,8},{8,16},{16,24},{1,9},{9,17},{17,25},{2,10},{10,18},{18,26},{... | collective-permute-start | bytes 1179656 | tf_op jit(solution)/shard_map/ppermute | solution.py:26
Sparse Core Ops, SparseCore 0:
  514.2 20.5 all-gather.1
where the time goes:
time: 571 us; the launch traced here: 566 us
  waiting for transfers between devices  137 us (24%)
  local copies, waits for them, and re-layouts  129 us (23%)
  matrix products  120 us (21%)
  blocking collectives  104 us (18%)
  other arithmetic  32.9 us (6%)
  starting transfers between devices  28.4 us (5%)
  between operations  14.8 us (3%)
    all_to_all x2, blocking collectives, on_device(): lax.all_to_all(near_modes, 'gy', split_axis=3, concat_axis=4, tiled=True)  104 us
    all_to_all x3, waiting for transfers between devices, on_device(): lax.all_to_all(back_rows, 'gy', split_axis=4, concat_axis=3, tiled=True)  64.3 us
    dot_general x3, matrix products, on_device(): jnp.einsum('lrcky,rkx->lcyx', own_modes, table_ix, preferred_element_type...  50.4 us
    unnamed x37, local copies, waits for them, and re-layouts  50 us
    all_to_all x1, waiting for transfers between devices, on_device(): lax.all_to_all(near_modes, 'gy', split_axis=3, concat_axis=4, tiled=True)  42.9 us
    dot_general x3, matrix products, on_device(): jnp.einsum('lcyx,co->loyx', current, point_weight, preferred_element_type...  39.6 us
    convert_element_type x3, local copies, waits for them, and re-layouts, on_device(): back_rows = jnp.einsum('klqcm,qmry->lrcky', mixed, table_iy, preferred_el...  27.5 us
    all_to_all x3, local copies, waits for them, and re-layouts, on_device(): lax.all_to_all(back_rows, 'gy', split_axis=4, concat_axis=3, tiled=True)  25.5 us
  transfers between devices with their start and end apart: 8, of which 8 were waited for; matrix products, arithmetic and copies ran while one was open for 8% of the time, Pallas kernels for 0%

commit v1 on v0

--- a/solution.py
+++ b/solution.py
@@ -119,7 +119,10 @@
         near_modes = jnp.einsum(
             "lcyx,rxk->lrcky", current, table_fx, preferred_element_type=jnp.float32
         ).astype(jnp.bfloat16)
-        all_rows = lax.all_to_all(near_modes, "gy", split_axis=3, concat_axis=4, tiled=True)
+        devices = lax.axis_size("gy")
+        blocks = jnp.stack(jnp.split(near_modes, devices, axis=3), axis=0)
+        blocks = lax.all_to_all(blocks, "gy", split_axis=0, concat_axis=0)
+        all_rows = jnp.concatenate(blocks, axis=4)
         table_fy = forward_y(every_row, total_rows, ymode_count)
         spectrum = jnp.einsum(
             "lrcky,ryqm->klqcm", all_rows, table_fy, preferred_element_type=jnp.float32

time: 571 us -> 643 us (1.13)
  local copies, waits for them, and re-layouts: 129 us -> 198 us
    another operation x3 -> x36, local copies, waits for them, and re-layouts: 7.97 us -> 75.1 us  [the longest x30 61.5 us: on_device(): blocks = jnp.stack(jnp.split(near_modes, devices, axis=3), axis=0)]
    unnamed x37 -> x120, local copies, waits for them, and re-layouts: 50 us -> 67.1 us
    convert_element_type x3 -> x0, local copies, waits for them, and re-layouts: 9.67 us -> none  [on_device(): near_modes = jnp.einsum('lcyx,rxk->lrcky', current, table_fx, preferred_e...]
  transfers between devices with their start and end apart: 8 -> 8, of which waited for: 8 -> 8; matrix products, arithmetic and copies ran while one was open for 8% -> 7% of each run, Pallas kernels for 0% -> 0%
where the time goes in v1:
time: 643 us; the launch traced here: 636 us
  local copies, waits for them, and re-layouts  198 us (31%)
  waiting for transfers between devices  138 us (21%)
  matrix products  120 us (19%)
  blocking collectives  104 us (16%)
  other arithmetic  32.4 us (5%)
  starting transfers between devices  28.3 us (4%)
  between operations  15.2 us (2%)
    all_to_all x2, blocking collectives, on_device(): blocks = lax.all_to_all(blocks, 'gy', split_axis=0, concat_axis=0)  104 us
    unnamed x120, local copies, waits for them, and re-layouts  67.1 us
    all_to_all x3, waiting for transfers between devices, on_device(): lax.all_to_all(back_rows, 'gy', split_axis=4, concat_axis=3, tiled=True)  65.4 us
    another operation x30, local copies, waits for them, and re-layouts, on_device(): blocks = jnp.stack(jnp.split(near_modes, devices, axis=3), axis=0)  61.5 us
    dot_general x3, matrix products, on_device(): jnp.einsum('lrcky,rkx->lcyx', own_modes, table_ix, preferred_element_type...  53.1 us
    all_to_all x1, waiting for transfers between devices, on_device(): blocks = lax.all_to_all(blocks, 'gy', split_axis=0, concat_axis=0)  42.9 us
    dot_general x3, matrix products, on_device(): jnp.einsum('lcyx,co->loyx', current, point_weight, preferred_element_type...  39.7 us
    convert_element_type x3, local copies, waits for them, and re-layouts, on_device(): back_rows = jnp.einsum('klqcm,qmry->lrcky', mixed, table_iy, preferred_el...  27.5 us
  transfers between devices with their start and end apart: 8, of which 8 were waited for; matrix products, arithmetic and copies ran while one was open for 7% of the time, Pallas kernels for 0%

profile of v1, /device:TPU:1, one launch (start us, length us, event | category | flops | bytes accessed | tf_op | source)
XLA Modules:
  0.0 635.8 jit_solution(3613972186984817604)
XLA Ops:
  14.8 5.1 slice_bitcast_fusion.16
  41.1 6.9 %all-to-all-start = ((bf16[8,1,2,32,16,96]{5,4,3,2,1,0:T(8,128)(2,1)}), bf16[8,1,2,32,16,96]{5,4,3,2,1,0:T(8,128)(2,1)S(1)}, u32[]{:S(2)}, u32[]{:S(2)}) async-start(bf16[8,1,2,32,16,96]{5,4,3,2,1,0:T(8,128)(2,1)} %constant_dynamic-update-slice_fusion), calls=%async_computation | async-start | bytes 4194304 | tf_op jit(solution)/shard_map/all_to_all | solution.py:124
  52.5 42.9 %all-to-all-done = bf16[8,1,2,32,16,96]{5,4,3,2,1,0:T(8,128)(2,1)S(1)} async-done(((bf16[8,1,2,32,16,96]{5,4,3,2,1,0:T(8,128)(2,1)}), bf16[8,1,2,32,16,96]{5,4,3,2,1,0:T(8,128)(2,1)S(1)}, u32[]{:S(2)}, u32[]{:S(2)}) %all-to-all-start) | async-done | bytes 1572896 | tf_op jit(solution)/shard_map/all_to_all | solution.py:124
  110.4 9.2 %copy.147 = bf16[1,2,32,16,768]{2,3,1,0,4:T(8,128)(2,1)} copy(bf16[1,2,32,16,768]{4,2,3,1,0:T(8,128)(2,1)S(1)} %fusion.58) | data formatting | bytes 3145728 | tf_op jit(solution)/shard_map/convert_element_type | solution.py:134
  119.5 9.5 %reshape.774 = bf16[8,2,49152]{2,1,0:T(2,128)(2,1)} reshape(bf16[768,1,2,16,32]{4,3,2,1,0:T(8,128)(2,1)} %bitcast.410) | data formatting | bytes 3145728
  136.2 16.5 %fusion.47 = f32[32,96,1024]{2,0,1:T(8,128)} fusion(bf16[32,96,1024]{2,1,0:T(8,128)(2,1)} %bitcast.425, bf16[32,32]{1,0:T(8,128)(2,1)S(1)} %copy-done), kind=kOutput, calls=%fused_computation.70 | convolution fusion | flops 201326592 | bytes 18876416 | tf_op jit(solution)/shard_map/lcyx,co->loyx/dot_general | solution.py:139
  152.7 17.6 %all-to-all-done.1 = bf16[8,2,49152]{2,1,0:T(2,128)(2,1)S(1)} async-done(((bf16[8,2,49152]{2,1,0:T(2,128)(2,1)}), bf16[8,2,49152]{2,1,0:T(2,128)(2,1)S(1)}, u32[]{:S(2)}, u32[]{:S(2)}) %all-to-all-start.1) | async-done | bytes 1572896 | tf_op jit(solution)/shard_map/all_to_all | solution.py:135
  170.2 5.4 reshape.775
  175.6 8.5 %copy.148 = bf16[1,2,32,16,8,96]{5,3,4,2,1,0:T(8,128)(2,1)S(1)} copy(bf16[1,2,32,16,8,96]{2,3,1,5,4,0:T(8,128)(2,1)} %bitcast.411) | data formatting | bytes 3145728 | tf_op jit(solution)/shard_map/all_to_all | solution.py:135
  184.2 17.8 %fusion.7 = bf16[1,32,96,1024]{3,2,1,0:T(8,128)(2,1)S(1)} fusion(f32[32,96,1024]{2,0,1:T(8,128)} %fusion.47, bf16[1,32,96,1024]{3,2,1,0:T(8,128)(2,1)} %param.9, f32[32]{0:T(128)S(1)} %copy-done.44, bf16[2,32,128,96]{3,2,1,0:T(8,128)(2,1)S(1)} %bitcast.429, bf16[1,128,1024]{2,1,0:T(8,128)(2,1)S(1)} %get-tuple-element.188, ...), kind=kOutput, calls=%fused_computation.23 | convolution fusion | flops 1651769344 | bytes 27263104 | tf_op jit(solution)/shard_map/lrcky,rkx->lcyx/dot_general | solution.py:136
  204.6 5.1 slice_bitcast_fusion.8
  231.4 51.7 %all_to_all.60 = bf16[8,1,2,32,16,96]{5,4,3,2,1,0:T(8,128)(2,1)S(1)} all-to-all(bf16[8,1,2,32,16,96]{5,4,3,2,1,0:T(8,128)(2,1)} %constant_dynamic-update-slice_fusion.8), channel_id=1, replica_groups=mesh['lev'=4,'gy'=8] {'gy'}, dimensions={0} | all-to-all | bytes 3145728 | tf_op jit(solution)/shard_map/all_to_all | solution.py:124
  289.2 5.2 fusion.33
  295.1 9.2 %copy.163 = bf16[1,2,32,16,768]{2,3,1,0,4:T(8,128)(2,1)} copy(bf16[1,2,32,16,768]{4,2,3,1,0:T(8,128)(2,1)S(1)} %fusion.59) | data formatting | bytes 3145728 | tf_op jit(solution)/shard_map/convert_element_type | solution.py:134
  304.3 9.5 %reshape.776 = bf16[8,2,49152]{2,1,0:T(2,128)(2,1)} reshape(bf16[768,1,2,16,32]{4,3,2,1,0:T(8,128)(2,1)} %bitcast.412) | data formatting | bytes 3145728
  318.0 11.6 %fusion.45 = f32[96,1024,32]{1,2,0:T(8,128)} fusion(bf16[32,96,1024]{2,1,0:T(8,128)(2,1)} %bitcast.427, bf16[32,32]{1,0:T(8,128)(2,1)S(1)} %copy-done), kind=kOutput, calls=%fused_computation.68 | convolution fusion | flops 201326592 | bytes 18876416 | tf_op jit(solution)/shard_map/lcyx,co->loyx/dot_general | solution.py:139
  329.6 24.2 %all-to-all-done.3 = bf16[8,2,49152]{2,1,0:T(2,128)(2,1)S(1)} async-done(((bf16[8,2,49152]{2,1,0:T(2,128)(2,1)}), bf16[8,2,49152]{2,1,0:T(2,128)(2,1)S(1)}, u32[]{:S(2)}, u32[]{:S(2)}) %all-to-all-start.3) | async-done | bytes 1572896 | tf_op jit(solution)/shard_map/all_to_all | solution.py:135
  353.9 5.4 reshape.777
  359.2 8.6 %copy.164 = bf16[1,2,32,16,8,96]{5,3,4,2,1,0:T(8,128)(2,1)S(1)} copy(bf16[1,2,32,16,8,96]{2,3,1,5,4,0:T(8,128)(2,1)} %bitcast.413) | data formatting | bytes 3145728 | tf_op jit(solution)/shard_map/all_to_all | solution.py:135
  367.8 17.7 %fusion.15 = bf16[1,32,96,1024]{3,2,1,0:T(8,128)(2,1)S(1)} fusion(f32[96,1024,32]{1,2,0:T(8,128)} %fusion.45, bf16[1,32,96,1024]{3,2,1,0:T(8,128)(2,1)} %param.9, f32[32]{0:T(128)S(1)} %copy-done.44, bf16[2,32,128,96]{3,2,1,0:T(8,128)(2,1)S(1)} %bitcast.430, bf16[1,128,1024]{2,1,0:T(8,128)(2,1)S(1)} %copy-done.36, bf16[1,128,1024]{2,1,0:T(8,128)(2,1)S(1)} %copy-done.39), kind=kOutput, calls=%fused_computation.31 | convolution fusion | flops 1651769344 | bytes 27263104 | tf_op jit(solution)/shard_map/lrcky,rkx->lcyx/dot_general | solution.py:136
  388.3 5.1 slice_bitcast_fusion
  414.8 52.2 %all_to_all.61 = bf16[8,1,2,32,16,96]{5,4,3,2,1,0:T(8,128)(2,1)S(1)} all-to-all(bf16[8,1,2,32,16,96]{5,4,3,2,1,0:T(8,128)(2,1)} %constant_dynamic-update-slice_fusion.16), channel_id=1, replica_groups=mesh['lev'=4,'gy'=8] {'gy'}, dimensions={0} | all-to-all | bytes 3145728 | tf_op jit(solution)/shard_map/all_to_all | solution.py:124
  473.1 5.2 fusion.35
  479.0 9.2 %copy.179 = bf16[1,2,32,16,768]{2,3,1,0,4:T(8,128)(2,1)} copy(bf16[1,2,32,16,768]{4,2,3,1,0:T(8,128)(2,1)S(1)} %fusion.60) | data formatting | bytes 3145728 | tf_op jit(solution)/shard_map/convert_element_type | solution.py:134
  488.1 9.5 %reshape.778 = bf16[8,2,49152]{2,1,0:T(2,128)(2,1)} reshape(bf16[768,1,2,16,32]{4,3,2,1,0:T(8,128)(2,1)} %bitcast.414) | data formatting | bytes 3145728
  502.7 11.6 %fusion.43 = f32[96,1024,32]{1,2,0:T(8,128)} fusion(bf16[32,96,1024]{2,1,0:T(8,128)(2,1)} %bitcast.426, bf16[32,32]{1,0:T(8,128)(2,1)S(1)} %copy-done), kind=kOutput, calls=%fused_computation.66 | convolution fusion | flops 201326592 | bytes 18876416 | tf_op jit(solution)/shard_map/lcyx,co->loyx/dot_general | solution.py:139
  514.3 23.6 %all-to-all-done.5 = bf16[8,2,49152]{2,1,0:T(2,128)(2,1)S(1)} async-done(((bf16[8,2,49152]{2,1,0:T(2,128)(2,1)}), bf16[8,2,49152]{2,1,0:T(2,128)(2,1)S(1)}, u32[]{:S(2)}, u32[]{:S(2)}) %all-to-all-start.5) | async-done | bytes 1572896 | tf_op jit(solution)/shard_map/all_to_all | solution.py:135
  537.9 5.8 reshape.779
  543.7 8.6 %copy.180 = bf16[1,2,32,16,8,96]{5,3,4,2,1,0:T(8,128)(2,1)S(1)} copy(bf16[1,2,32,16,8,96]{2,3,1,5,4,0:T(8,128)(2,1)} %bitcast.415) | data formatting | bytes 3145728 | tf_op jit(solution)/shard_map/all_to_all | solution.py:135
  552.3 17.6 %fusion.22 = f32[1,32,96,1024]{3,2,1,0:T(8,128)S(1)} fusion(f32[96,1024,32]{1,2,0:T(8,128)} %fusion.43, bf16[1,32,96,1024]{3,2,1,0:T(8,128)(2,1)} %param.9, f32[32]{0:T(128)S(1)} %copy-done.44, bf16[2,32,128,96]{3,2,1,0:T(8,128)(2,1)S(1)} %bitcast.428, bf16[1,128,1024]{2,1,0:T(8,128)(2,1)S(1)} %copy-done.37, bf16[1,128,1024]{2,1,0:T(8,128)(2,1)S(1)} %copy-done.40), kind=kOutput, calls=%fused_computation.38 | convolution fusion | flops 1648623616 | bytes 33554560 | tf_op jit(solution)/shard_map/lrcky,rkx->lcyx/dot_general | solution.py:136
  569.9 11.3 %fusion.23 = f32[96,1024,4]{1,2,0:T(4,128)S(1)} fusion(f32[32,96,1024]{2,1,0:T(8,128)S(1)} %bitcast.421, bf16[4,32]{1,0:T(4,128)(2,1)S(1)} %copy-done.41), kind=kOutput, calls=%fused_computation.45 | convolution fusion | flops 150994944 | bytes 14156032 | tf_op jit(solution)/shard_map/lcyx,fc->flyx/dot_general | solution.py:144
  583.7 20.7 %all-gather.2.cloned.1.call-done = f32[4,96,1024]{2,1,0:T(8,128)} async-done(((f32[1,96,1024]{2,1,0:T(8,128)}), f32[4,96,1024]{2,1,0:T(8,128)}) %all-gather.2.cloned.1.call-update) | async-done | bytes 1572880 | tf_op jit(solution)/shard_map/all_gather | solution.py:12
  (202 shorter events, 157.4 us)
Async XLA Ops:
  7.2 129.0 %copy-start = (bf16[32,32]{1,0:T(8,128)(2,1)S(1)}, bf16[32,32]{1,0:T(8,128)(2,1)}, u32[]{:S(2)}) copy-start(bf16[32,32]{1,0:T(8,128)(2,1)} %param.11) | copy-start | bytes 6148
  41.1 54.3 %all-to-all-start = ((bf16[8,1,2,32,16,96]{5,4,3,2,1,0:T(8,128)(2,1)}), bf16[8,1,2,32,16,96]{5,4,3,2,1,0:T(8,128)(2,1)S(1)}, u32[]{:S(2)}, u32[]{:S(2)}) async-start(bf16[8,1,2,32,16,96]{5,4,3,2,1,0:T(8,128)(2,1)} %constant_dynamic-update-slice_fusion), calls=%async_computation | async-start | bytes 4194304 | tf_op jit(solution)/shard_map/all_to_all | solution.py:124
  50.6 51.7 %copy-start.24 = (bf16[1,768,2,128]{3,1,0,2:T(8,128)(2,1)}, bf16[1,768,2,128]{3,1,0,2:T(8,128)(2,1)S(1)}, u32[]{:S(2)}) copy-start(bf16[1,768,2,128]{3,1,0,2:T(8,128)(2,1)S(1)} %get-tuple-element.178) | copy-start | bytes 1179652
  52.5 57.3 %copy-start.18 = (bf16[1,128,2,768]{3,1,0,2:T(8,128)(2,1)}, bf16[1,128,2,768]{3,1,0,2:T(8,128)(2,1)S(1)}, u32[]{:S(2)}) copy-start(bf16[1,128,2,768]{3,1,0,2:T(8,128)(2,1)S(1)} %get-tuple-element.176) | copy-start | bytes 1179652
  52.5 57.3 %copy-start.21 = (bf16[1,128,2,768]{3,1,0,2:T(8,128)(2,1)}, bf16[1,128,2,768]{3,1,0,2:T(8,128)(2,1)S(1)}, u32[]{:S(2)}) copy-start(bf16[1,128,2,768]{3,1,0,2:T(8,128)(2,1)S(1)} %get-tuple-element.177) | copy-start | bytes 1179652
  129.1 41.2 %all-to-all-start.1 = ((bf16[8,2,49152]{2,1,0:T(2,128)(2,1)}), bf16[8,2,49152]{2,1,0:T(2,128)(2,1)S(1)}, u32[]{:S(2)}, u32[]{:S(2)}) async-start(bf16[8,2,49152]{2,1,0:T(2,128)(2,1)} %reshape.774), calls=%async_computation.1 | async-start | bytes 3145728 | tf_op jit(solution)/shard_map/all_to_all | solution.py:135
  136.1 48.0 %copy-start.35 = (bf16[1,128,1024]{2,1,0:T(8,128)(2,1)}, bf16[1,128,1024]{2,1,0:T(8,128)(2,1)S(1)}, u32[]{:S(2)}) copy-start(bf16[1,128,1024]{2,1,0:T(8,128)(2,1)S(1)} %get-tuple-element.188) | copy-start | bytes 786436
  136.1 48.0 %copy-start.38 = (bf16[1,128,1024]{2,1,0:T(8,128)(2,1)}, bf16[1,128,1024]{2,1,0:T(8,128)(2,1)S(1)}, u32[]{:S(2)}) copy-start(bf16[1,128,1024]{2,1,0:T(8,128)(2,1)S(1)} %get-tuple-element.189) | copy-start | bytes 786436
  175.6 8.5 %copy-start.44 = (f32[32]{0:T(128)S(1)}, f32[32]{0:T(128)}, u32[]{:S(2)}) copy-start(f32[32]{0:T(128)} %param.12) | copy-start | bytes 388
  184.1 17.8 %copy-start.30 = (bf16[1,1024,128]{2,1,0:T(8,128)(2,1)S(1)}, bf16[1,1024,128]{2,1,0:T(8,128)(2,1)}, u32[]{:S(2)}) copy-start(bf16[1,1024,128]{2,1,0:T(8,128)(2,1)} %copy-done.29) | copy-start | bytes 786436
  184.2 17.8 %copy-start.33 = (bf16[1,1024,128]{2,1,0:T(8,128)(2,1)S(1)}, bf16[1,1024,128]{2,1,0:T(8,128)(2,1)}, u32[]{:S(2)}) copy-start(bf16[1,1024,128]{2,1,0:T(8,128)(2,1)} %copy-done.32) | copy-start | bytes 786436
  224.3 5.0 copy-start.7
  289.2 5.3 copy-start.19
  289.2 5.3 copy-start.22
  313.8 40.1 %all-to-all-start.3 = ((bf16[8,2,49152]{2,1,0:T(2,128)(2,1)}), bf16[8,2,49152]{2,1,0:T(2,128)(2,1)S(1)}, u32[]{:S(2)}, u32[]{:S(2)}) async-start(bf16[8,2,49152]{2,1,0:T(2,128)(2,1)} %reshape.776), calls=%async_computation.3 | async-start | bytes 3145728 | tf_op jit(solution)/shard_map/all_to_all | solution.py:135
  359.2 8.6 %copy-start.36 = (bf16[1,128,1024]{2,1,0:T(8,128)(2,1)S(1)}, bf16[1,128,1024]{2,1,0:T(8,128)(2,1)}, u32[]{:S(2)}) copy-start(bf16[1,128,1024]{2,1,0:T(8,128)(2,1)} %copy-done.35) | copy-start | bytes 786436
  359.2 8.6 %copy-start.39 = (bf16[1,128,1024]{2,1,0:T(8,128)(2,1)S(1)}, bf16[1,128,1024]{2,1,0:T(8,128)(2,1)}, u32[]{:S(2)}) copy-start(bf16[1,128,1024]{2,1,0:T(8,128)(2,1)} %copy-done.38) | copy-start | bytes 786436
  367.8 17.8 %copy-start.31 = (bf16[1,1024,128]{2,1,0:T(8,128)(2,1)S(1)}, bf16[1,1024,128]{2,1,0:T(8,128)(2,1)}, u32[]{:S(2)}) copy-start(bf16[1,1024,128]{2,1,0:T(8,128)(2,1)} %copy-done.29) | copy-start | bytes 786436
  367.8 17.8 %copy-start.34 = (bf16[1,1024,128]{2,1,0:T(8,128)(2,1)S(1)}, bf16[1,1024,128]{2,1,0:T(8,128)(2,1)}, u32[]{:S(2)}) copy-start(bf16[1,1024,128]{2,1,0:T(8,128)(2,1)} %copy-done.32) | copy-start | bytes 786436
  407.9 4.7 copy-start.8
  473.1 5.3 copy-start.20
  473.1 5.3 copy-start.23
  497.6 40.2 %all-to-all-start.5 = ((bf16[8,2,49152]{2,1,0:T(2,128)(2,1)}), bf16[8,2,49152]{2,1,0:T(2,128)(2,1)S(1)}, u32[]{:S(2)}, u32[]{:S(2)}) async-start(bf16[8,2,49152]{2,1,0:T(2,128)(2,1)} %reshape.778), calls=%async_computation.5 | async-start | bytes 3145728 | tf_op jit(solution)/shard_map/all_to_all | solution.py:135
  502.0 102.4 %all-gather.2.cloned.1.call-start = ((), (), s32[]{:S(2)}) async-start(), calls=%async_computation.6 | async-start | bytes 1966080 | tf_op jit(solution)/shard_map/all_gather | solution.py:12
  543.7 8.6 %copy-start.37 = (bf16[1,128,1024]{2,1,0:T(8,128)(2,1)S(1)}, bf16[1,128,1024]{2,1,0:T(8,128)(2,1)}, u32[]{:S(2)}) copy-start(bf16[1,128,1024]{2,1,0:T(8,128)(2,1)} %copy-done.35) | copy-start | bytes 786436
  543.7 8.6 %copy-start.40 = (bf16[1,128,1024]{2,1,0:T(8,128)(2,1)S(1)}, bf16[1,128,1024]{2,1,0:T(8,128)(2,1)}, u32[]{:S(2)}) copy-start(bf16[1,128,1024]{2,1,0:T(8,128)(2,1)} %copy-done.38) | copy-start | bytes 786436
  552.2 17.6 %copy-start.41 = (bf16[4,32]{1,0:T(4,128)(2,1)S(1)}, bf16[4,32]{1,0:T(4,128)(2,1)}, u32[]{:S(2)}) copy-start(bf16[4,32]{1,0:T(4,128)(2,1)} %param.13) | copy-start | bytes 772
  569.9 11.3 %copy-start.1 = (f32[1,32,96,1024]{3,2,1,0:T(8,128)}, f32[1,32,96,1024]{3,2,1,0:T(8,128)S(1)}, u32[]{:S(2)}) copy-start(f32[1,32,96,1024]{3,2,1,0:T(8,128)S(1)} %fusion.22) | copy-start | bytes 37748740
  609.2 9.4 %copy-start.42 = (f32[96]{0:T(128)S(1)}, f32[96]{0:T(128)}, u32[]{:S(2)}) copy-start(f32[96]{0:T(128)} %param.14) | copy-start | bytes 1156
  609.2 4.8 collective-permute-start
  613.2 5.2 collective-permute-start.1
  618.9 8.5 %collective-permute-start.2 = (f32[96,1024]{1,0:T(8,128)S(1)}, f32[96,1024]{1,0:T(8,128)S(1)}, u32[]{:S(2)}, u32[]{:S(2)}) collective-permute-start(f32[96,1024]{1,0:T(8,128)S(1)} %get-tuple-element.135), channel_id=1, source_target_pairs={{0,8},{8,16},{16,24},{1,9},{9,17},{17,25},{2,10},{10,18},{18,26},{... | collective-permute-start | bytes 1179656 | tf_op jit(solution)/shard_map/ppermute | solution.py:26
  (21 other events, 62.4 us)
Sparse Core Ops, SparseCore 0:
  583.9 20.5 all-gather.1
